TPU v7x, 32 devices: a whole 2x2x4 slice. The times are simulated.
32 devices in a mesh: groups: 2 (over y), row: 16 (over z, x, core).
Axes of the slice: x: 2, y: 2, z: 4, core: 2. Of those that a mesh axis runs over, the one named last changes fastest.
Arguments:
- inputs: bfloat16 [32, 8192], P(('groups', 'row')), parts along dimension 0, may hold values from -6 to 6
- out_grad: bfloat16 [32, 8192], P(('groups', 'row')), parts along dimension 0, may hold values from -6 to 6
- gate_weight: bfloat16 [8192, 16384], P(None, 'row'), may hold values from -0.125 to 0.125
- up_weight: bfloat16 [8192, 16384], P(None, 'row'), may hold values from -0.09375 to 0.09375
- down_weight: bfloat16 [16384, 8192], P('row'), may hold values from -0.09375 to 0.09375
- block_mask: int32 [3, 128, 64], P(None, 'row'), may hold values from 0 to 1, as said below
Outputs:
- outputs: bfloat16 [32, 8192], P(('groups', 'row')), parts along dimension 0
- in_grad: bfloat16 [32, 8192], P(('groups', 'row')), parts along dimension 0
- gate_grad: bfloat16 [16384, 16384], P('groups', 'row'), parts along dimension 0
- up_grad: bfloat16 [16384, 16384], P('groups', 'row'), parts along dimension 0
- down_grad: bfloat16 [32768, 8192], P(('groups', 'row')), parts along dimension 0
There are 2 independent parts, one for each index of `groups`. A program takes and returns all parts, laid end to end along the dimension named above; an argument that names none is the same for every part. Nothing has to cross between parts.
Inputs may be any that keep to these rules, and one draw needn't show every extreme that they name: `block_mask`: each entry is 0 or 1. The share of kept blocks differs from hidden block to hidden block, about a quarter to three quarters.
All inputs are finite; a program needn't handle non-finite values.
Results may differ from a plain program's by a relative error of at most 0.005.
Values may be sent and summed in bfloat16 or wider, within the bound.
A program may use at most 256 MiB of HBM per device.

v0:
```python
import functools

import jax
import jax.numpy as jnp
from jax import lax
from jax.experimental import pallas as pl
from jax.experimental.pallas import tpu as pltpu
from jax.sharding import PartitionSpec as P

BLOCK = 128
SUB = 16
F32, BF16 = jnp.float32, jnp.bfloat16
VM = pltpu.VMEM
MIB = 1 << 20


def dot(a, b, ca=1, cb=0):
    return lax.dot_general(a, b, (((ca,), (cb,)), ((), ())), preferred_element_type=F32)


def spread(rows, cols):
    at = lax.broadcasted_iota(jnp.int32, (rows, cols), 1) // BLOCK
    return (at == lax.broadcasted_iota(jnp.int32, (rows, cols), 0)).astype(BF16)


def diagonal(v, tokens, nb):
    return jnp.concatenate(
        [v[b * tokens:(b + 1) * tokens, b * BLOCK:(b + 1) * BLOCK] for b in range(nb)], axis=1
    )


def layer(n, fc, mine_ref, mask_ref, wg_hbm, wu_hbm, wd_hbm,
          out_ref, hid_ref, gd_ref, ud_ref, x_ref, o_ref, md_ref, mfg_ref, mfu_ref,
          wg, wu, wd, meg, meu, mfd, xm, yacc, iacc, got, part, from_core, chip_sum, from_chips,
          wsem, dsem, gsend, grecv, fsend, csem, rsend, rrecv):
    d = x_ref.shape[1]
    f = hid_ref.shape[1]
    nch = f // fc
    nb = fc // BLOCK
    fb = f // BLOCK
    db = d // BLOCK
    chips = n // 2
    lanes = d // SUB
    me = lax.axis_index("row")
    grp = lax.axis_index("groups")
    chip, core = me // 2, lax.rem(me, 2)
    sib = chip * 2 + (1 - core)

    def weight_copies(c):
        cols = pl.ds(pl.multiple_of(c * fc, fc), fc)
        return (
            pltpu.make_async_copy(wg_hbm.at[:, cols], wg.at[c], wsem.at[0, c]),
            pltpu.make_async_copy(wu_hbm.at[:, cols], wu.at[c], wsem.at[1, c]),
            pltpu.make_async_copy(wd_hbm.at[cols, :], wd.at[c], wsem.at[2, c]),
        )

    for c in range(nch):
        for cp in weight_copies(c):
            cp.start()

    barrier = pltpu.get_barrier_semaphore()

    def peer(j):
        return lax.rem(chip + j, chips)

    def signal(j, carry):
        pl.semaphore_signal(barrier, inc=1, device_id=(grp, peer(j) * 2 + core),
                            device_id_type=pl.DeviceIdType.MESH)
        return carry

    lax.fori_loop(1, chips, signal, 0)
    pl.semaphore_signal(barrier, inc=1, device_id=(grp, sib), device_id_type=pl.DeviceIdType.MESH)
    pl.semaphore_wait(barrier, chips)

    def row_to(j):
        q = peer(j)
        return pltpu.make_async_remote_copy(
            src_ref=mine_ref, dst_ref=got.at[me], send_sem=gsend.at[q], recv_sem=grecv.at[me],
            device_id=(grp, q * 2 + core), device_id_type=pl.DeviceIdType.MESH)

    def row_from(j):
        q = peer(j)
        return pltpu.make_async_remote_copy(
            src_ref=mine_ref, dst_ref=got.at[q * 2 + core], send_sem=gsend.at[q],
            recv_sem=grecv.at[q * 2 + core],
            device_id=(grp, q * 2 + core), device_id_type=pl.DeviceIdType.MESH)

    def forward(j):
        q = peer(j)
        return pltpu.make_async_remote_copy(
            src_ref=got.at[q * 2 + core], dst_ref=got.at[q * 2 + core], send_sem=fsend.at[q],
            recv_sem=grecv.at[q * 2 + core],
            device_id=(grp, sib), device_id_type=pl.DeviceIdType.MESH)

    def forwarded(j):
        q = peer(j)
        return pltpu.make_async_remote_copy(
            src_ref=got.at[q * 2 + 1 - core], dst_ref=got.at[q * 2 + 1 - core],
            send_sem=fsend.at[q], recv_sem=grecv.at[q * 2 + 1 - core],
            device_id=(grp, sib), device_id_type=pl.DeviceIdType.MESH)

    own_to_sib = pltpu.make_async_remote_copy(
        src_ref=mine_ref, dst_ref=got.at[me], send_sem=fsend.at[chip], recv_sem=grecv.at[me],
        device_id=(grp, sib), device_id_type=pl.DeviceIdType.MESH)

    def start_row(j, carry):
        row_to(j).start()
        return carry

    lax.fori_loop(1, chips, start_row, 0)
    own_to_sib.start()
    got[me] = mine_ref[...]

    over_d = spread(db, d)
    over_f = spread(fb, f)
    keep = [mask_ref[k].astype(F32).astype(BF16) for k in range(3)]
    meg[...] = dot(keep[0], over_d)
    meu[...] = dot(keep[1], over_d)
    md_ref[...] = dot(keep[2], over_d)
    mfg_ref[...] = dot(keep[0], over_f, 0, 0)
    mfu_ref[...] = dot(keep[1], over_f, 0, 0)
    mfd[...] = dot(keep[2], over_f, 0, 0)
    yacc[...] = jnp.zeros_like(yacc)
    iacc[...] = jnp.zeros_like(iacc)
    side = SUB * SUB
    at_r = lax.broadcasted_iota(jnp.int32, (side, side), 0)
    at_c = lax.broadcasted_iota(jnp.int32, (side, side), 1)
    swap = (at_c == (at_r % SUB) * SUB + at_r // SUB).astype(BF16)

    def pass_on(j, carry):
        row_from(j).wait_recv()
        forward(j).start()
        return carry

    lax.fori_loop(1, chips, pass_on, 0)

    def take(j, carry):
        forwarded(j).wait_recv()
        return carry

    lax.fori_loop(0, chips, take, 0)

    for g in range(n // SUB):
        for k, whole in ((0, x_ref), (1, o_ref)):
            v = got[g * SUB:(g + 1) * SUB, k].reshape(side, lanes)
            v = dot(swap, v).astype(BF16)
            for s in range(SUB):
                whole[g * SUB:(g + 1) * SUB, s * lanes:(s + 1) * lanes] = v[s * SUB:(s + 1) * SUB]

    width = 2 * BLOCK

    def masked_rows(src, mref, c):
        for b in range(nb):
            row = mref[pl.ds(c * nb + b, 1), :].astype(BF16)
            xm[b * n:(b + 1) * n, :] = src[...] * row

    def chunk(c, carry):
        cols = pl.ds(pl.multiple_of(c * fc, fc), fc)
        cg, cu, cd = weight_copies(c)
        masked_rows(x_ref, meg, c)
        cg.wait()
        gate = diagonal(dot(xm[...], wg[c]), n, nb)
        masked_rows(x_ref, meu, c)
        cu.wait()
        up = diagonal(dot(xm[...], wu[c]), n, nb)
        masked_rows(o_ref, md_ref, c)
        cd.wait()
        hg = diagonal(dot(xm[...], wd[c], 1, 1), n, nb)
        sig = jax.nn.sigmoid(gate)
        hid = (gate * sig * up).astype(BF16)
        gd = (hg * up * sig * (1.0 + gate * (1.0 - sig))).astype(BF16)
        ud = (hg * gate * sig).astype(BF16)
        hid_ref[:, cols] = hid
        gd_ref[:, cols] = gd
        ud_ref[:, cols] = ud

        def stacked(v, mref, j):
            return jnp.concatenate(
                [v * mref[pl.ds(2 * j + b, 1), cols].astype(BF16) for b in range(2)], axis=0)

        def feature(j, carry):
            dc = pl.ds(pl.multiple_of(j * width, width), width)
            y = dot(stacked(hid, mfd, j), wd[c, :, dc])
            yacc[:, dc] += diagonal(y, n, 2)
            i = dot(stacked(gd, mfg_ref, j), wg[c, dc, :], 1, 1)
            i += dot(stacked(ud, mfu_ref, j), wu[c, dc, :], 1, 1)
            iacc[:, dc] += diagonal(i, n, 2)
            return carry

        lax.fori_loop(0, d // width, feature, 0, unroll=4)
        return carry

    lax.fori_loop(0, nch, chunk, 0)

    for g in range(n // SUB):
        for k, acc in ((0, yacc), (1, iacc)):
            v = jnp.concatenate(
                [acc[g * SUB:(g + 1) * SUB, s * lanes:(s + 1) * lanes] for s in range(SUB)],
                axis=0).astype(BF16)
            v = dot(swap, v).astype(BF16)
            for t in range(SUB):
                part[t % 2, g * (SUB // 2) + t // 2, k] = v[t * SUB:(t + 1) * SUB]

    swap_cores = pltpu.make_async_remote_copy(
        src_ref=part.at[1 - core], dst_ref=from_core, send_sem=csem.at[0], recv_sem=csem.at[1],
        device_id=(grp, sib), device_id_type=pl.DeviceIdType.MESH)
    swap_cores.start()
    swap_cores.wait()

    def to_chip(j):
        q = peer(j)
        return pltpu.make_async_remote_copy(
            src_ref=chip_sum.at[q], dst_ref=from_chips.at[chip], send_sem=rsend.at[q],
            recv_sem=rrecv.at[chip],
            device_id=(grp, q * 2 + core), device_id_type=pl.DeviceIdType.MESH)

    def from_chip(j):
        q = peer(j)
        return pltpu.make_async_remote_copy(
            src_ref=chip_sum.at[q], dst_ref=from_chips.at[q], send_sem=rsend.at[q],
            recv_sem=rrecv.at[q],
            device_id=(grp, q * 2 + core), device_id_type=pl.DeviceIdType.MESH)

    def send_sum(j, carry):
        q = peer(j)
        chip_sum[q] = (part[core, q].astype(F32) + from_core[q].astype(F32)).astype(BF16)
        to_chip(j).start()
        return carry

    lax.fori_loop(1, chips, send_sum, 0)
    total = part[core, chip].astype(F32) + from_core[chip].astype(F32)

    def add_sum(j, total):
        from_chip(j).wait_recv()
        return total + from_chips[peer(j)].astype(F32)

    total = lax.fori_loop(1, chips, add_sum, total)
    out_ref[...] = total.astype(BF16)

    def drain(j, carry):
        row_to(j).wait_send()
        forward(j).wait_send()
        to_chip(j).wait_send()
        return carry

    lax.fori_loop(1, chips, drain, 0)
    own_to_sib.wait_send()


def grads(x_ref, o_ref, hid_ref, gd_ref, ud_ref, md_ref, mfg_ref, mfu_ref,
          gg_ref, ug_ref, dg_ref):
    i = pl.program_id(0)
    rows = gg_ref.shape[0]
    blocks = rows // BLOCK
    for b in range(blocks):
        at = slice(b * BLOCK, (b + 1) * BLOCK)
        xb = x_ref[:, at]
        row = pl.ds(i * blocks + b, 1)
        gg_ref[at, :] = dot(xb, gd_ref[...] * mfg_ref[row, :].astype(BF16), 0, 0).astype(BF16)
        ug_ref[at, :] = dot(xb, ud_ref[...] * mfu_ref[row, :].astype(BF16), 0, 0).astype(BF16)
    hid = hid_ref[...]
    d = o_ref.shape[1]
    step = min(d, 1024)
    for c in range(d // step):
        at = slice(c * step, (c + 1) * step)
        og = o_ref[:, at] * md_ref[pl.ds(i, 1), at].astype(BF16)
        dg_ref[:, at] = dot(hid, og, 0, 0).astype(BF16)


def per_device(n, inputs, out_grad, gate_weight, up_weight, down_weight, block_mask):
    d, f = gate_weight.shape
    fc = min(f, 2 * BLOCK)
    nch = f // fc
    nb = fc // BLOCK
    fb, db = f // BLOCK, d // BLOCK
    chips = n // 2
    lanes = d // SUB
    mine = jnp.concatenate([inputs, out_grad], axis=0).reshape(2, SUB, lanes)
    vmem = pl.BlockSpec(memory_space=pltpu.VMEM)
    hbm = pl.BlockSpec(memory_space=pl.ANY)
    S = jax.ShapeDtypeStruct
    dma = pltpu.SemaphoreType.DMA
    out, hid, gd, ud, x, o, md, mfg, mfu = pl.pallas_call(
        functools.partial(layer, n, fc),
        out_shape=(S((2, SUB, lanes), BF16), S((n, f), BF16), S((n, f), BF16), S((n, f), BF16),
                   S((n, d), BF16), S((n, d), BF16), S((fb, d), F32), S((db, f), F32),
                   S((db, f), F32)),
        in_specs=[vmem, vmem, hbm, hbm, hbm],
        out_specs=(vmem,) * 9,
        scratch_shapes=[
            VM((nch, d, fc), BF16), VM((nch, d, fc), BF16), VM((nch, fc, d), BF16),
            VM((fb, d), F32), VM((fb, d), F32), VM((db, f), F32), VM((nb * n, d), BF16),
            VM((n, d), F32), VM((n, d), F32),
            VM((n, 2, SUB, lanes), BF16), VM((2, chips, 2, SUB, lanes), BF16),
            VM((chips, 2, SUB, lanes), BF16), VM((chips, 2, SUB, lanes), BF16),
            VM((chips, 2, SUB, lanes), BF16),
            dma((3, nch)), dma((1,)), dma((chips,)), dma((n,)), dma((chips,)), dma((2,)),
            dma((chips,)), dma((chips,)),
        ],
        compiler_params=pltpu.CompilerParams(
            collective_id=0, has_side_effects=True, vmem_limit_bytes=61 * MIB),
        name="layer",
    )(mine, block_mask, gate_weight, up_weight, down_weight)

    rows = d // fb
    full = lambda *shape: pl.BlockSpec(shape, lambda i: (0,) * len(shape))
    gg, ug, dg = pl.pallas_call(
        grads,
        grid=(fb,),
        out_shape=(S((d, f), BF16), S((d, f), BF16), S((f, d), BF16)),
        in_specs=[pl.BlockSpec((n, rows), lambda i: (0, i)), full(n, d),
                  pl.BlockSpec((n, BLOCK), lambda i: (0, i)), full(n, f), full(n, f),
                  full(fb, d), full(db, f), full(db, f)],
        out_specs=(pl.BlockSpec((rows, f), lambda i: (i, 0)),
                   pl.BlockSpec((rows, f), lambda i: (i, 0)),
                   pl.BlockSpec((BLOCK, d), lambda i: (i, 0))),
        compiler_params=pltpu.CompilerParams(vmem_limit_bytes=48 * MIB),
        name="grads",
    )(x, o, hid, gd, ud, md, mfg, mfu)
    out = out.reshape(2, d)
    return out[0:1], out[1:2], gg, ug, dg


def solution(mesh):
    in_specs = (
        P(("groups", "row"), None),
        P(("groups", "row"), None),
        P(None, "row"),
        P(None, "row"),
        P("row", None),
        P(None, "row", None),
    )
    out_specs = (
        P(("groups", "row"), None),
        P(("groups", "row"), None),
        P("groups", "row"),
        P("groups", "row"),
        P(("groups", "row"), None),
    )
    return jax.shard_map(
        functools.partial(per_device, mesh.shape["row"]),
        mesh=mesh, in_specs=in_specs, out_specs=out_specs, check_vma=False,
    )
```

profile of v0, /device:TPU:0, one launch (start us, length us, event | category | flops | bytes accessed | tf_op | source)
XLA Modules:
  0.0 84.4 jit_solution(12357224654694562578)
XLA Ops:
  0.6 0.9 %pad_maximum_fusion = bf16[2,8192]{1,0:T(2,128)(2,1)S(1)} fusion(bf16[1,8192]{1,0:T(2,128)(2,1)} %param.7, bf16[1,8192]{1,0:T(2,128)(2,1)} %param.6), kind=kLoop, calls=%fused_computation.1 | loop fusion | flops 65536 | bytes 65536 | tf_op jit(solution)/shard_map/concatenate | solution.py:278
  1.5 0.6 copy.15
  2.1 55.8 %layer.1 = (bf16[2,16,512]{2,1,0:T(8,128)(2,1)}, bf16[16,1024]{1,0:T(8,128)(2,1)}, bf16[16,1024]{1,0:T(8,128)(2,1)}, bf16[16,1024]{1,0:T(8,128)(2,1)}, bf16[16,8...) custom-call(bf16[2,16,512]{2,1,0:T(8,128)(2,1)} %bitcast.10, ...), custom_call_target="tpu_custom_call" | custom-call | tf_op jit(solution)/shard_map/layer/pallas_call | solution.py:283
  57.9 0.0 copy-start
  57.9 0.9 %copy-done = bf16[16,8192]{1,0:T(8,128)(2,1)S(1)} copy-done((bf16[16,8192]{1,0:T(8,128)(2,1)S(1)}, bf16[16,8192]{1,0:T(8,128)(2,1)}, u32[]{:S(2)}) %copy-start) | copy-done | bytes 262168
  58.9 0.0 copy-start.1
  58.9 0.9 %copy-done.1 = bf16[16,8192]{1,0:T(8,128)(2,1)S(1)} copy-done((bf16[16,8192]{1,0:T(8,128)(2,1)S(1)}, bf16[16,8192]{1,0:T(8,128)(2,1)}, u32[]{:S(2)}) %copy-start.1) | copy-done | bytes 262168
  59.8 0.0 copy-start.2
  59.8 0.9 %copy-done.2 = f32[8,8192]{1,0:T(8,128)S(1)} copy-done((f32[8,8192]{1,0:T(8,128)S(1)}, f32[8,8192]{1,0:T(8,128)}, u32[]{:S(2)}) %copy-start.2) | copy-done | bytes 262168
  60.8 0.0 copy-start.3
  60.8 0.9 %copy-done.3 = f32[64,1024]{1,0:T(8,128)S(1)} copy-done((f32[64,1024]{1,0:T(8,128)S(1)}, f32[64,1024]{1,0:T(8,128)}, u32[]{:S(2)}) %copy-start.3) | copy-done | bytes 262168
  61.7 0.0 copy-start.4
  61.7 0.9 %copy-done.4 = f32[64,1024]{1,0:T(8,128)S(1)} copy-done((f32[64,1024]{1,0:T(8,128)S(1)}, f32[64,1024]{1,0:T(8,128)}, u32[]{:S(2)}) %copy-start.4) | copy-done | bytes 262168
  62.7 0.0 copy-start.5
  62.7 0.8 copy-done.5
  63.4 0.0 copy-start.6
  63.4 0.8 copy-done.6
  64.2 0.0 copy-start.7
  64.2 0.8 copy-done.7
  64.9 17.5 %grads.1 = (bf16[8192,1024]{1,0:T(8,128)(2,1)}, bf16[8192,1024]{1,0:T(8,128)(2,1)}, bf16[1024,8192]{1,0:T(8,128)(2,1)}) custom-call(bf16[16,8192]{1,0:T(8,128)(2,1)S(1)} %copy-done, bf16[16,8192]{1,0:T(8,128)(2,1)S(1)} %copy-done.1, bf16[16,1024]{1,0:T(8,128)(2,1)S(1)} %copy-done.5, bf16[16,1024]{1,0:T(8,128)(2,1)S(1)} %copy-done.6, ...), custom_call_target="tpu_custom_call" | custom-call | tf_op jit(solution)/shard_map/grads/pallas_call | solution.py:307
  82.4 0.7 slice_bitcast_fusion
  83.1 0.6 copy.12
  83.8 0.6 copy.13
Async XLA Ops:
  57.9 1.0 %copy-start = (bf16[16,8192]{1,0:T(8,128)(2,1)S(1)}, bf16[16,8192]{1,0:T(8,128)(2,1)}, u32[]{:S(2)}) copy-start(bf16[16,8192]{1,0:T(8,128)(2,1)} %get-tuple-element.18.x_ref) | copy-start | bytes 786436
  58.9 0.9 %copy-start.1 = (bf16[16,8192]{1,0:T(8,128)(2,1)S(1)}, bf16[16,8192]{1,0:T(8,128)(2,1)}, u32[]{:S(2)}) copy-start(bf16[16,8192]{1,0:T(8,128)(2,1)} %get-tuple-element.19.o_ref) | copy-start | bytes 786436
  59.8 0.9 %copy-start.2 = (f32[8,8192]{1,0:T(8,128)S(1)}, f32[8,8192]{1,0:T(8,128)}, u32[]{:S(2)}) copy-start(f32[8,8192]{1,0:T(8,128)} %get-tuple-element.23.md_ref) | copy-start | bytes 786436
  60.8 0.9 %copy-start.3 = (f32[64,1024]{1,0:T(8,128)S(1)}, f32[64,1024]{1,0:T(8,128)}, u32[]{:S(2)}) copy-start(f32[64,1024]{1,0:T(8,128)} %get-tuple-element.24.mfg_ref) | copy-start | bytes 786436
  61.7 0.9 %copy-start.4 = (f32[64,1024]{1,0:T(8,128)S(1)}, f32[64,1024]{1,0:T(8,128)}, u32[]{:S(2)}) copy-start(f32[64,1024]{1,0:T(8,128)} %get-tuple-element.25.mfu_ref) | copy-start | bytes 786436
  62.7 0.8 copy-start.5
  63.4 0.8 copy-start.6
  64.2 0.8 copy-start.7
where the time goes:
time: 85.1 us; the launch traced here: 84.4 us
  Pallas kernels  73.3 us (86%)
  local copies, waits for them, and re-layouts  9.65 us (11%)
    pallas_call x1, Pallas kernels, per_device(): pl.pallas_call(functools.partial(layer, n, fc), out_shape=(S((2, SUB, lan...  55.8 us
    pallas_call x1, Pallas kernels, per_device(): pl.pallas_call(grads, grid=(fb,), out_shape=(S((d, f), BF16), S((d, f), B...  17.5 us
    unnamed x20, local copies, waits for them, and re-layouts  9.65 us

commit v1 on v0

--- a/solution.py
+++ b/solution.py
@@ -120,8 +120,6 @@
     mfg_ref[...] = dot(keep[0], over_f, 0, 0)
     mfu_ref[...] = dot(keep[1], over_f, 0, 0)
     mfd[...] = dot(keep[2], over_f, 0, 0)
-    yacc[...] = jnp.zeros_like(yacc)
-    iacc[...] = jnp.zeros_like(iacc)
     side = SUB * SUB
     at_r = lax.broadcasted_iota(jnp.int32, (side, side), 0)
     at_c = lax.broadcasted_iota(jnp.int32, (side, side), 1)
@@ -165,7 +163,7 @@
         up = diagonal(dot(xm[...], wu[c]), n, nb)
         masked_rows(o_ref, md_ref, c)
         cd.wait()
-        hg = diagonal(dot(xm[...], wd[c], 1, 1), n, nb)
+        hg = diagonal(dot(wd[c], xm[...], 1, 1).T, n, nb)
         sig = jax.nn.sigmoid(gate)
         hid = (gate * sig * up).astype(BF16)
         gd = (hg * up * sig * (1.0 + gate * (1.0 - sig))).astype(BF16)
@@ -174,73 +172,99 @@
         gd_ref[:, cols] = gd
         ud_ref[:, cols] = ud
 
-        def stacked(v, mref, j):
-            return jnp.concatenate(
-                [v * mref[pl.ds(2 * j + b, 1), cols].astype(BF16) for b in range(2)], axis=0)
-
-        def feature(j, carry):
-            dc = pl.ds(pl.multiple_of(j * width, width), width)
-            y = dot(stacked(hid, mfd, j), wd[c, :, dc])
-            yacc[:, dc] += diagonal(y, n, 2)
-            i = dot(stacked(gd, mfg_ref, j), wg[c, dc, :], 1, 1)
-            i += dot(stacked(ud, mfu_ref, j), wu[c, dc, :], 1, 1)
-            iacc[:, dc] += diagonal(i, n, 2)
-            return carry
-
-        lax.fori_loop(0, d // width, feature, 0, unroll=4)
         return carry
 
     lax.fori_loop(0, nch, chunk, 0)
 
-    for g in range(n // SUB):
-        for k, acc in ((0, yacc), (1, iacc)):
+    def stacked(ref, mref, j, c):
+        cols = slice(c * fc, (c + 1) * fc)
+        return jnp.concatenate(
+            [ref[:, cols] * mref[pl.ds(2 * j + b, 1), cols].astype(BF16) for b in range(2)], axis=0)
+
+    def y_feature(j, carry):
+        dc = pl.ds(pl.multiple_of(j * width, width), width)
+        y = dot(stacked(hid_ref, mfd, j, 0), wd[0, :, dc])
+        for c in range(1, nch):
+            y += dot(stacked(hid_ref, mfd, j, c), wd[c, :, dc])
+        yacc[:, dc] = diagonal(y, n, 2)
+        return carry
+
+    def in_feature(j, carry):
+        dc = pl.ds(pl.multiple_of(j * width, width), width)
+        i = dot(stacked(gd_ref, mfg_ref, j, 0), wg[0, dc, :], 1, 1)
+        for c in range(1, nch):
+            i += dot(stacked(gd_ref, mfg_ref, j, c), wg[c, dc, :], 1, 1)
+        for c in range(nch):
+            i += dot(stacked(ud_ref, mfu_ref, j, c), wu[c, dc, :], 1, 1)
+        iacc[:, dc] = diagonal(i, n, 2)
+        return carry
+
+    def pack(k, acc):
+        for g in range(n // SUB):
             v = jnp.concatenate(
                 [acc[g * SUB:(g + 1) * SUB, s * lanes:(s + 1) * lanes] for s in range(SUB)],
                 axis=0).astype(BF16)
             v = dot(swap, v).astype(BF16)
             for t in range(SUB):
-                part[t % 2, g * (SUB // 2) + t // 2, k] = v[t * SUB:(t + 1) * SUB]
-
-    swap_cores = pltpu.make_async_remote_copy(
-        src_ref=part.at[1 - core], dst_ref=from_core, send_sem=csem.at[0], recv_sem=csem.at[1],
-        device_id=(grp, sib), device_id_type=pl.DeviceIdType.MESH)
-    swap_cores.start()
-    swap_cores.wait()
-
-    def to_chip(j):
-        q = peer(j)
-        return pltpu.make_async_remote_copy(
-            src_ref=chip_sum.at[q], dst_ref=from_chips.at[chip], send_sem=rsend.at[q],
-            recv_sem=rrecv.at[chip],
+                part[t % 2, k, g * (SUB // 2) + t // 2] = v[t * SUB:(t + 1) * SUB]
+
+    def swap_cores(k):
+        return pltpu.make_async_remote_copy(
+            src_ref=part.at[1 - core, k], dst_ref=from_core.at[k], send_sem=csem.at[k, 0],
+            recv_sem=csem.at[k, 1],
+            device_id=(grp, sib), device_id_type=pl.DeviceIdType.MESH)
+
+    def to_chip(k, j):
+        q = peer(j)
+        return pltpu.make_async_remote_copy(
+            src_ref=chip_sum.at[k, q], dst_ref=from_chips.at[k, chip], send_sem=rsend.at[k, q],
+            recv_sem=rrecv.at[k, chip],
             device_id=(grp, q * 2 + core), device_id_type=pl.DeviceIdType.MESH)
 
-    def from_chip(j):
-        q = peer(j)
-        return pltpu.make_async_remote_copy(
-            src_ref=chip_sum.at[q], dst_ref=from_chips.at[q], send_sem=rsend.at[q],
-            recv_sem=rrecv.at[q],
+    def from_chip(k, j):
+        q = peer(j)
+        return pltpu.make_async_remote_copy(
+            src_ref=chip_sum.at[k, q], dst_ref=from_chips.at[k, q], send_sem=rsend.at[k, q],
+            recv_sem=rrecv.at[k, q],
             device_id=(grp, q * 2 + core), device_id_type=pl.DeviceIdType.MESH)
 
-    def send_sum(j, carry):
-        q = peer(j)
-        chip_sum[q] = (part[core, q].astype(F32) + from_core[q].astype(F32)).astype(BF16)
-        to_chip(j).start()
-        return carry
-
-    lax.fori_loop(1, chips, send_sum, 0)
-    total = part[core, chip].astype(F32) + from_core[chip].astype(F32)
-
-    def add_sum(j, total):
-        from_chip(j).wait_recv()
-        return total + from_chips[peer(j)].astype(F32)
-
-    total = lax.fori_loop(1, chips, add_sum, total)
-    out_ref[...] = total.astype(BF16)
+    def send_sums(k):
+        swap_cores(k).wait()
+
+        def send_sum(j, carry):
+            q = peer(j)
+            chip_sum[k, q] = (part[core, k, q].astype(F32) + from_core[k, q].astype(F32)).astype(BF16)
+            to_chip(k, j).start()
+            return carry
+
+        lax.fori_loop(1, chips, send_sum, 0)
+
+    def finish(k):
+        def add_sum(j, total):
+            from_chip(k, j).wait_recv()
+            return total + from_chips[k, peer(j)].astype(F32)
+
+        total = part[core, k, chip].astype(F32) + from_core[k, chip].astype(F32)
+        out_ref[k] = lax.fori_loop(1, chips, add_sum, total).astype(BF16)
+
+    tiles = d // width
+    lax.fori_loop(0, tiles, y_feature, 0, unroll=4)
+    pack(0, yacc)
+    swap_cores(0).start()
+    lax.fori_loop(0, tiles // 4, in_feature, 0, unroll=2)
+    send_sums(0)
+    lax.fori_loop(tiles // 4, tiles, in_feature, 0, unroll=2)
+    pack(1, iacc)
+    swap_cores(1).start()
+    send_sums(1)
+    finish(0)
+    finish(1)
 
     def drain(j, carry):
         row_to(j).wait_send()
         forward(j).wait_send()
-        to_chip(j).wait_send()
+        to_chip(0, j).wait_send()
+        to_chip(1, j).wait_send()
         return carry
 
     lax.fori_loop(1, chips, drain, 0)
@@ -291,11 +315,11 @@
             VM((nch, d, fc), BF16), VM((nch, d, fc), BF16), VM((nch, fc, d), BF16),
             VM((fb, d), F32), VM((fb, d), F32), VM((db, f), F32), VM((nb * n, d), BF16),
             VM((n, d), F32), VM((n, d), F32),
-            VM((n, 2, SUB, lanes), BF16), VM((2, chips, 2, SUB, lanes), BF16),
-            VM((chips, 2, SUB, lanes), BF16), VM((chips, 2, SUB, lanes), BF16),
-            VM((chips, 2, SUB, lanes), BF16),
-            dma((3, nch)), dma((1,)), dma((chips,)), dma((n,)), dma((chips,)), dma((2,)),
-            dma((chips,)), dma((chips,)),
+            VM((n, 2, SUB, lanes), BF16), VM((2, 2, chips, SUB, lanes), BF16),
+            VM((2, chips, SUB, lanes), BF16), VM((2, chips, SUB, lanes), BF16),
+            VM((2, chips, SUB, lanes), BF16),
+            dma((3, nch)), dma((1,)), dma((chips,)), dma((n,)), dma((chips,)), dma((2, 2)),
+            dma((2, chips)), dma((2, chips)),
         ],
         compiler_params=pltpu.CompilerParams(
             collective_id=0, has_side_effects=True, vmem_limit_bytes=61 * MIB),
@@ -314,7 +338,7 @@
         out_specs=(pl.BlockSpec((rows, f), lambda i: (i, 0)),
                    pl.BlockSpec((rows, f), lambda i: (i, 0)),
                    pl.BlockSpec((BLOCK, d), lambda i: (i, 0))),
-        compiler_params=pltpu.CompilerParams(vmem_limit_bytes=48 * MIB),
+        compiler_params=pltpu.CompilerParams(vmem_limit_bytes=61 * MIB),
         name="grads",
     )(x, o, hid, gd, ud, md, mfg, mfu)
     out = out.reshape(2, d)

time: 85.1 us -> 77.7 us (0.913)
  local copies, waits for them, and re-layouts: 9.65 us -> 2.64 us
    unnamed x20 -> x4, local copies, waits for them, and re-layouts: 9.65 us -> 2.64 us
    pallas_call x1, Pallas kernels: 55.8 us -> 54.8 us  [per_device(): pl.pallas_call(functools.partial(layer, n, fc), out_shape=(S((2, SUB, lan...]
    pallas_call x1, Pallas kernels: 17.5 us -> 18.5 us  [per_device(): pl.pallas_call(grads, grid=(fb,), out_shape=(S((d, f), BF16), S((d, f), B...]
where the time goes in v1:
time: 77.7 us; the launch traced here: 77.4 us
  Pallas kernels  73.3 us (94%)
  local copies, waits for them, and re-layouts  2.64 us (3%)
  other arithmetic  0.85 us (1%)
    pallas_call x1, Pallas kernels, per_device(): pl.pallas_call(functools.partial(layer, n, fc), out_shape=(S((2, SUB, lan...  54.8 us
    pallas_call x1, Pallas kernels, per_device(): pl.pallas_call(grads, grid=(fb,), out_shape=(S((d, f), BF16), S((d, f), B...  18.5 us
    unnamed x4, local copies, waits for them, and re-layouts  2.64 us

profile of v1, /device:TPU:0, one launch (start us, length us, event | category | flops | bytes accessed | tf_op | source)
XLA Modules:
  0.0 77.4 jit_solution(12820472302570370912)
XLA Ops:
  0.6 0.9 %pad_maximum_fusion = bf16[2,8192]{1,0:T(2,128)(2,1)S(1)} fusion(bf16[1,8192]{1,0:T(2,128)(2,1)} %param.7, bf16[1,8192]{1,0:T(2,128)(2,1)} %param.6), kind=kLoop, calls=%fused_computation.1 | loop fusion | flops 65536 | bytes 65536 | tf_op jit(solution)/shard_map/concatenate | solution.py:302
  1.5 0.6 copy.15
  2.1 54.8 %layer.1 = (bf16[2,16,512]{2,1,0:T(8,128)(2,1)}, bf16[16,1024]{1,0:T(8,128)(2,1)}, bf16[16,1024]{1,0:T(8,128)(2,1)}, bf16[16,1024]{1,0:T(8,128)(2,1)}, bf16[16,8...) custom-call(bf16[2,16,512]{2,1,0:T(8,128)(2,1)} %bitcast.10, ...), custom_call_target="tpu_custom_call" | custom-call | tf_op jit(solution)/shard_map/layer/pallas_call | solution.py:307
  56.9 18.5 %grads.1 = (bf16[8192,1024]{1,0:T(8,128)(2,1)}, bf16[8192,1024]{1,0:T(8,128)(2,1)}, bf16[1024,8192]{1,0:T(8,128)(2,1)}) custom-call(bf16[16,8192]{1,0:T(8,128)(2,1)} %get-tuple-element.18.x_ref, bf16[16,8192]{1,0:T(8,128)(2,1)} %get-tuple-element.19.o_ref, bf16[16,1024]{1,0:T(8,128)(2,1)} %get-tuple-element.20.hid_ref, ...), custom_call_target="tpu_custom_call" | custom-call | tf_op jit(solution)/shard_map/grads/pallas_call | solution.py:331
  75.4 0.7 slice_bitcast_fusion
  76.1 0.6 copy.12
  76.8 0.6 copy.13
